TPU v7x, 256 devices: a whole 4x4x8 slice. The times are simulated.
256 devices in a mesh: req: 64 (over z, x, core), tp: 4 (over y).
Axes of the slice: x: 4, y: 4, z: 8, core: 2. Of those that a mesh axis runs over, the one named last changes fastest.
Arguments:
- hidden: bfloat16 [2048, 5120], P('req', 'tp'), may hold values from -8 to 8
- gain: float32 [5120], replicated, may hold values from 0.5 to 1.5
- head_weight: bfloat16 [5120, 131072], P(None, ('req', 'tp')), may hold values from -0.3 to 0.3
- token_ids: int32 [2048], P('req'), may hold values from 0 to 131071
- lengths: int32 [64], P('req'), may hold values from 1 to 32, as said below
- owner_device: int32 [64], replicated, may hold values from 0 to 63, each once
Outputs:
- logprob: float32 [2048], P('req')
- entropy: float32 [2048], P('req')
Inputs may be any that keep to these rules, and one draw needn't show every extreme that they name: `lengths`: each sequence has 1 to 32 live slots; some sequence has exactly 32. `owner_device`: A permutation of the req indices.
All inputs are finite; a program needn't handle non-finite values.
Results may differ from a plain program's by a relative error of at most 0.0041.
Values may be sent and summed in bfloat16 or wider, within the bound.
No kernel may reach another device: no remote copies, remote signals or barrier semaphores. Data moves between devices by JAX's collectives and lax.ppermute only.
A program may use at most 128 MiB of HBM per device.

v0:
```python
import math
import jax
import jax.numpy as jnp
from jax import lax
from jax.sharding import PartitionSpec as P


def finalize(peak_logit, exp_total, exp_spread, pick_logit):
    log_total = peak_logit + jnp.log(exp_total)
    return (pick_logit - log_total, log_total - exp_spread / exp_total)


def score_rows(all_rows, all_ids, columns, vocab_base):
    row_total = all_rows.shape[0]
    block_rows = math.gcd(row_total, 256)
    row_blocks = all_rows.reshape(row_total // block_rows, block_rows, all_rows.shape[1])
    id_blocks = all_ids.reshape(row_total // block_rows, block_rows)

    def score_block(block_args):
        piece_rows, piece_ids = block_args
        logits = jnp.dot(piece_rows, columns, preferred_element_type=jnp.float32)
        peak_logit = jnp.max(logits, axis=-1)
        weights_exp = jnp.exp(logits - peak_logit[:, None])
        exp_total = jnp.sum(weights_exp, axis=-1)
        exp_spread = jnp.sum(weights_exp * logits, axis=-1)
        vocab_index = vocab_base + lax.broadcasted_iota(jnp.int32, logits.shape, 1)
        pick_logit = jnp.sum(jnp.where(piece_ids[:, None] == vocab_index, logits, 0.0), axis=-1)
        return (peak_logit, exp_total, exp_spread, pick_logit)

    stats = lax.map(score_block, (row_blocks, id_blocks))
    return tuple((member.reshape(-1) for member in stats))


def local(hidden, gain, head_weight, token_ids, lengths, owner_device):
    gathered = lax.all_gather(hidden, "tp", axis=1, tiled=True)
    values = gathered.astype(jnp.float32)
    mean_square = jnp.mean(values * values, axis=-1, keepdims=True)
    normed = (values * lax.rsqrt(mean_square + 1e-05) * gain).astype(jnp.bfloat16)
    seq_slots = normed.shape[0]
    tp_count = lax.axis_size("tp")
    req_count = lax.axis_size("req")
    vocab_base = (lax.axis_index("req") * tp_count + lax.axis_index("tp")) * head_weight.shape[1]
    all_rows, all_ids = (
        lax.all_gather(normed, "req", axis=0, tiled=True),
        lax.all_gather(token_ids, "req", axis=0, tiled=True),
    )
    stats = score_rows(all_rows, all_ids, head_weight, vocab_base)
    global_peak = lax.pmax(stats[0], ("req", "tp"))
    rescale = jnp.exp(stats[0] - global_peak)
    exp_total, exp_spread, pick_logit = lax.psum(
        (stats[1] * rescale, stats[2] * rescale, stats[3]), ("req", "tp")
    )
    stats = (global_peak, exp_total, exp_spread, pick_logit)
    row_logprob, row_entropy = finalize(*stats)
    row_logprob = row_logprob.reshape(req_count, seq_slots)
    row_entropy = row_entropy.reshape(req_count, seq_slots)
    worker = owner_device[lax.axis_index("req")]
    own_logprob = lax.dynamic_index_in_dim(row_logprob, worker, 0, keepdims=False)
    own_entropy = lax.dynamic_index_in_dim(row_entropy, worker, 0, keepdims=False)
    live_mask = jnp.arange(seq_slots, dtype=jnp.int32) < lengths[0]
    return (jnp.where(live_mask, own_logprob, 0.0), jnp.where(live_mask, own_entropy, 0.0))


def solution(mesh):
    placed = (P("req", "tp"), P(), P(None, ("req", "tp")), P("req"), P("req"), P())
    return jax.shard_map(
        local, mesh=mesh, in_specs=placed, out_specs=(P("req"), P("req")), check_vma=False
    )
```

profile of v0, /device:TPU:1, one launch (start us, length us, event | category | flops | bytes accessed | tf_op | source)
XLA Modules:
  0.0 335.5 jit_solution(15491374336734146777)
XLA Ops:
  7.2 0.0 all-gather.2.cloned.1.call-start
  7.2 11.9 %all_gather.9 = bf16[32,5120]{1,0:T(8,128)(2,1)S(1)} all-gather(bf16[32,1280]{1,0:T(8,128)(2,1)} %param.8), channel_id=1, replica_groups=mesh['req'=64,'tp'=4] {'tp'}, dimensions={1}, use_global_device_ids=true | all-gather | bytes 409600 | tf_op jit(solution)/shard_map/all_gather | solution.py:35
  19.1 0.2 fusion.5
  19.3 1.6 fusion.7
  20.9 0.0 all-gather.2.cloned.1.call-update
  21.0 1.3 dynamic_slice.18
  23.5 1.3 dynamic-slice
  25.4 0.9 dynamic-update-slice
  26.3 22.6 %all-reduce = s32[2048]{0:T(1024)S(1)} all-reduce(s32[2048]{0:T(1024)S(1)} %dynamic-update-slice), channel_id=1, replica_groups=mesh['req'=64,'tp'=4] {'req'}, use_global_device_ids=true, to_apply=%add | all-reduce | flops 2048 | bytes 16384
  50.2 85.8 %all-gather.2.cloned.1.call-done = bf16[2048,5120]{1,0:T(8,128)(2,1)} async-done(((bf16[32,5120]{1,0:T(8,128)(2,1)}), bf16[2048,5120]{1,0:T(8,128)(2,1)}) %all-gather.2.cloned.1.call-update) | async-done | bytes 20971536 | tf_op jit(solution)/shard_map/all_gather | solution.py:44
  136.0 43.6 %while.16 = (s32[]{:T(128)}, f32[8,256]{1,0:T(8,128)S(1)}, f32[8,256]{1,0:T(8,128)S(1)}, f32[8,256]{1,0:T(8,128)S(1)}, f32[8,256]{1,0:T(8,128)S(1)}, /*index=5*/...) while((s32[]{:T(128)}, f32[8,256]{1,0:T(8,128)S(1)}, ...), condition=%wide.region_6.7_spmd, body=%wide.region_1.6_spmd.sunk | while | flops 1343225344 | bytes 8934021 | solution.py:30
  136.0 4.9 %fusion.16 = (f32[256]{0:T(256)S(1)}, f32[256,512]{1,0:T(8,128)S(1)}) fusion(bf16[5120,512]{1,0:T(8,128)(2,1)} %get-tuple-element.181, bf16[8,256,5120]{2,1,0:T(8,128)(2,1)} %get-tuple-element.180, s32[]{:T(128)} %get-tuple-element.164), kind=kOutput, calls=%fused_computation.24.clone.1 | convolution fusion | flops 1342308096 | bytes 8390144 | tf_op jit(solution)/shard_map/while/body/eval_jaxpr/dot_general | solution.py:21
  140.9 0.3 multiply_reduce_fusion.2
  141.5 4.9 %fusion.16 = (f32[256]{0:T(256)S(1)}, f32[256,512]{1,0:T(8,128)S(1)}) fusion(bf16[5120,512]{1,0:T(8,128)(2,1)} %get-tuple-element.181, bf16[8,256,5120]{2,1,0:T(8,128)(2,1)} %get-tuple-element.180, s32[]{:T(128)} %get-tuple-element.164), kind=kOutput, calls=%fused_computation.24.clone.1 | convolution fusion | flops 1342308096 | bytes 8390144 | tf_op jit(solution)/shard_map/while/body/eval_jaxpr/dot_general | solution.py:21
  146.4 0.3 multiply_reduce_fusion.2
  146.9 4.9 %fusion.16 = (f32[256]{0:T(256)S(1)}, f32[256,512]{1,0:T(8,128)S(1)}) fusion(bf16[5120,512]{1,0:T(8,128)(2,1)} %get-tuple-element.181, bf16[8,256,5120]{2,1,0:T(8,128)(2,1)} %get-tuple-element.180, s32[]{:T(128)} %get-tuple-element.164), kind=kOutput, calls=%fused_computation.24.clone.1 | convolution fusion | flops 1342308096 | bytes 8390144 | tf_op jit(solution)/shard_map/while/body/eval_jaxpr/dot_general | solution.py:21
  151.8 0.3 multiply_reduce_fusion.2
  152.4 4.9 %fusion.16 = (f32[256]{0:T(256)S(1)}, f32[256,512]{1,0:T(8,128)S(1)}) fusion(bf16[5120,512]{1,0:T(8,128)(2,1)} %get-tuple-element.181, bf16[8,256,5120]{2,1,0:T(8,128)(2,1)} %get-tuple-element.180, s32[]{:T(128)} %get-tuple-element.164), kind=kOutput, calls=%fused_computation.24.clone.1 | convolution fusion | flops 1342308096 | bytes 8390144 | tf_op jit(solution)/shard_map/while/body/eval_jaxpr/dot_general | solution.py:21
  157.3 0.3 multiply_reduce_fusion.2
  157.8 4.9 %fusion.16 = (f32[256]{0:T(256)S(1)}, f32[256,512]{1,0:T(8,128)S(1)}) fusion(bf16[5120,512]{1,0:T(8,128)(2,1)} %get-tuple-element.181, bf16[8,256,5120]{2,1,0:T(8,128)(2,1)} %get-tuple-element.180, s32[]{:T(128)} %get-tuple-element.164), kind=kOutput, calls=%fused_computation.24.clone.1 | convolution fusion | flops 1342308096 | bytes 8390144 | tf_op jit(solution)/shard_map/while/body/eval_jaxpr/dot_general | solution.py:21
  162.7 0.3 multiply_reduce_fusion.2
  163.3 4.9 %fusion.16 = (f32[256]{0:T(256)S(1)}, f32[256,512]{1,0:T(8,128)S(1)}) fusion(bf16[5120,512]{1,0:T(8,128)(2,1)} %get-tuple-element.181, bf16[8,256,5120]{2,1,0:T(8,128)(2,1)} %get-tuple-element.180, s32[]{:T(128)} %get-tuple-element.164), kind=kOutput, calls=%fused_computation.24.clone.1 | convolution fusion | flops 1342308096 | bytes 8390144 | tf_op jit(solution)/shard_map/while/body/eval_jaxpr/dot_general | solution.py:21
  168.2 0.3 multiply_reduce_fusion.2
  168.7 4.9 %fusion.16 = (f32[256]{0:T(256)S(1)}, f32[256,512]{1,0:T(8,128)S(1)}) fusion(bf16[5120,512]{1,0:T(8,128)(2,1)} %get-tuple-element.181, bf16[8,256,5120]{2,1,0:T(8,128)(2,1)} %get-tuple-element.180, s32[]{:T(128)} %get-tuple-element.164), kind=kOutput, calls=%fused_computation.24.clone.1 | convolution fusion | flops 1342308096 | bytes 8390144 | tf_op jit(solution)/shard_map/while/body/eval_jaxpr/dot_general | solution.py:21
  173.6 0.3 multiply_reduce_fusion.2
  174.2 4.9 %fusion.16 = (f32[256]{0:T(256)S(1)}, f32[256,512]{1,0:T(8,128)S(1)}) fusion(bf16[5120,512]{1,0:T(8,128)(2,1)} %get-tuple-element.181, bf16[8,256,5120]{2,1,0:T(8,128)(2,1)} %get-tuple-element.180, s32[]{:T(128)} %get-tuple-element.164), kind=kOutput, calls=%fused_computation.24.clone.1 | convolution fusion | flops 1342308096 | bytes 8390144 | tf_op jit(solution)/shard_map/while/body/eval_jaxpr/dot_general | solution.py:21
  179.1 0.3 multiply_reduce_fusion.2
  179.7 74.6 %pmax.7 = f32[2048]{0:T(1024)S(1)} all-reduce(f32[2048]{0:T(1024)S(1)} %bitcast.47), channel_id=1, replica_groups=mesh['req'=64,'tp'=4] {'req','tp'}, use_global_device_ids=true, to_apply=%region_8.9 | all-reduce | flops 2048 | bytes 16384 | tf_op jit(solution)/shard_map/pmax | solution.py:48
  254.3 73.7 %all-reduce.1 = (f32[2048]{0:T(1024)S(1)}, f32[2048]{0:T(1024)S(1)}, f32[2048]{0:T(1024)S(1)}) all-reduce(f32[2048]{0:T(1024)S(1)} %bitcast.49, f32[2048]{0:T(1024)S(1)} %get-tuple-element.85, f32[2048]{0:T(1024)S(1)} %get-tuple-element.84), channel_id=1, replica_groups=mesh['req'=64,'tp'=4] {'req','tp'}, use_global_device_ids=true, to_apply=%region_7.8 | all-reduce | flops 6144 | bytes 49152 | tf_op jit(solution)/shard_map/psum | solution.py:50
  328.0 0.1 reshape.45
  328.1 0.1 reshape.47
  328.1 0.5 compare_select_fusion
  (61 shorter events, 1.5 us)
Async XLA Ops:
  7.2 128.8 %all-gather.2.cloned.1.call-start = ((), (), s32[]{:S(2)}) async-start(), calls=%async_computation | async-start | bytes 21299200 | tf_op jit(solution)/shard_map/all_gather | solution.py:44
Sparse Core Ops, SparseCore 0:
  21.0 114.9 all-gather.1
where the time goes:
time: 336 us; the launch traced here: 335 us
  blocking collectives  183 us (54%)
  waiting for transfers between devices  85.8 us (26%)
  matrix products  39 us (12%)
  between operations  17.3 us (5%)
  other arithmetic  5.12 us (2%)
  local copies, waits for them, and re-layouts  4.96 us (1%)
    all_gather x1, waiting for transfers between devices, local(): lax.all_gather(normed, 'req', axis=0, tiled=True)  85.8 us
    pmax x1, blocking collectives, local(): global_peak = lax.pmax(stats[0], ('req', 'tp'))  74.6 us
    psum x1, blocking collectives, local(): lax.psum((stats[1] * rescale, stats[2] * rescale, stats[3]), ('req', 'tp'))  73.7 us
    dot_general x8, matrix products, score_block(): logits = jnp.dot(piece_rows, columns, preferred_element_type=jnp.float32)  39 us
    unnamed x1, blocking collectives  22.6 us
    all_gather x1, blocking collectives, local(): gathered = lax.all_gather(hidden, 'tp', axis=1, tiled=True)  11.9 us
  transfers between devices with their start and end apart: 1, of which 1 were waited for; matrix products, arithmetic and copies ran while one was open for 1% of the time, Pallas kernels for 0%

commit v1 on v0

--- a/solution.py
+++ b/solution.py
@@ -1,8 +1,18 @@
+import functools
 import math
 import jax
 import jax.numpy as jnp
 from jax import lax
 from jax.sharding import PartitionSpec as P
+
+
+def write_the_loads(local_block, shard_axis):
+    s_next = jnp.stack(lax.axis_size(shard_axis) * [local_block])
+    r2 = lax.all_to_all(s_next, axis_name=shard_axis, split_axis=0, concat_axis=0)
+    return jnp.concatenate(r2, axis=0)
+
+
+expand_frames_on_mesh = functools.partial(write_the_loads, shard_axis="req")
 
 
 def finalize(peak_logit, exp_total, exp_spread, pick_logit):
@@ -41,7 +51,7 @@
     req_count = lax.axis_size("req")
     vocab_base = (lax.axis_index("req") * tp_count + lax.axis_index("tp")) * head_weight.shape[1]
     all_rows, all_ids = (
-        lax.all_gather(normed, "req", axis=0, tiled=True),
+        expand_frames_on_mesh(normed),
         lax.all_gather(token_ids, "req", axis=0, tiled=True),
     )
     stats = score_rows(all_rows, all_ids, head_weight, vocab_base)

time: 336 us -> 701 us (2.09)
  blocking collectives: 183 us -> 628 us
  waiting for transfers between devices: 85.8 us -> 0.01 us
  starting transfers between devices: 0.04 us -> 14.5 us
  between operations: 17.3 us -> 4.1 us
    unnamed x1, blocking collectives: 22.6 us -> 463 us
    all_gather x1 -> x0, waiting for transfers between devices: 85.8 us -> none  [local(): lax.all_gather(normed, 'req', axis=0, tiled=True)]
    all_to_all x0 -> x1, starting transfers between devices: none -> 14.5 us  [write_the_loads(): lax.all_to_all(s_next, axis_name=shard_axis, split_axis=0, concat_axis=0)]
    another operation x0 -> x1, local copies, waits for them, and re-layouts: none -> 7.4 us  [write_the_loads(): s_next = jnp.stack(lax.axis_size(shard_axis) * [local_block])]
  transfers between devices with their start and end apart: 1 -> 1, of which waited for: 1 -> 0; matrix products, arithmetic and copies ran while one was open for 1% -> 0% of each run, Pallas kernels for 0% -> 0%
where the time goes in v1:
time: 701 us
  blocking collectives  628 us (90%)
  matrix products  39 us (6%)
  starting transfers between devices  14.5 us (2%)
  local copies, waits for them, and re-layouts  10.5 us (1%)
    unnamed x1, blocking collectives  463 us
    pmax x1, blocking collectives, local(): global_peak = lax.pmax(stats[0], ('req', 'tp'))  78.8 us
    psum x1, blocking collectives, local(): lax.psum((stats[1] * rescale, stats[2] * rescale, stats[3]), ('req', 'tp'))  73.9 us
    dot_general x8, matrix products, score_block(): logits = jnp.dot(piece_rows, columns, preferred_element_type=jnp.float32)  39 us
    all_to_all x1, starting transfers between devices, write_the_loads(): lax.all_to_all(s_next, axis_name=shard_axis, split_axis=0, concat_axis=0)  14.5 us
  transfers between devices with their start and end apart: 1, of which 0 were waited for; matrix products, arithmetic and copies ran while one was open for 0% of the time, Pallas kernels for 0%

profile of v1, /device:TPU:1, one launch (start us, length us, event | category | flops | bytes accessed | tf_op | source)
XLA Modules:
  0.0 700.8 jit_solution(14837446633777553902)
XLA Ops:
  0.6 11.9 %all_gather.6 = bf16[32,5120]{1,0:T(8,128)(2,1)S(1)} all-gather(bf16[32,1280]{1,0:T(8,128)(2,1)} %param.8), channel_id=1, replica_groups=mesh['req'=64,'tp'=4] {'tp'}, dimensions={1}, use_global_device_ids=true | all-gather | bytes 409600 | tf_op jit(solution)/shard_map/all_gather | solution.py:45
  12.5 0.2 fusion.5
  12.7 0.9 fusion.7
  13.6 7.4 %stack.2 = bf16[64,32,5120]{2,1,0:T(8,128)(2,1)} broadcast(bf16[32,5120]{1,0:T(8,128)(2,1)S(1)} %fusion.7), dimensions={1,2} | broadcast | bytes 21299200 | tf_op jit(solution)/shard_map/stack | solution.py:10
  21.0 0.0 copy-start
  21.0 0.0 copy-start.2
  21.0 0.0 copy-start.1
  21.0 14.5 %all-to-all-start = ((bf16[64,32,5120]{2,1,0:T(8,128)(2,1)}), bf16[64,32,5120]{2,1,0:T(8,128)(2,1)}, u32[]{:S(2)}, u32[]{:S(2)}) async-start(bf16[64,32,5120]{2,1,0:T(8,128)(2,1)} %stack.2), calls=%async_computation | async-start | bytes 41943040 | tf_op jit(solution)/shard_map/all_to_all | solution.py:11
  35.6 0.0 copy-done
  35.6 0.6 dynamic_slice.18
  37.6 0.0 copy-done.2
  37.6 0.6 dynamic-slice
  38.8 0.0 copy-done.1
  38.8 0.3 dynamic-update-slice
  39.1 463.3 %all-reduce = s32[2048]{0:T(1024)S(1)} all-reduce(s32[2048]{0:T(1024)S(1)} %dynamic-update-slice), channel_id=1, replica_groups=mesh['req'=64,'tp'=4] {'req'}, use_global_device_ids=true, to_apply=%add | all-reduce | flops 2048 | bytes 16384
  503.8 0.0 all-to-all-done
  503.8 43.6 %while.16 = (s32[]{:T(128)}, f32[8,256]{1,0:T(8,128)S(1)}, f32[8,256]{1,0:T(8,128)S(1)}, f32[8,256]{1,0:T(8,128)S(1)}, f32[8,256]{1,0:T(8,128)S(1)}, /*index=5*/...) while((s32[]{:T(128)}, f32[8,256]{1,0:T(8,128)S(1)}, ...), condition=%wide.region_6.7_spmd, body=%wide.region_1.6_spmd.sunk | while | flops 1343225344 | bytes 8934021 | solution.py:40
  503.8 4.9 fusion.16
  508.7 0.3 multiply_reduce_fusion.2
  509.2 4.9 fusion.16
  514.1 0.3 multiply_reduce_fusion.2
  514.7 4.9 fusion.16
  519.6 0.3 multiply_reduce_fusion.2
  520.1 4.9 fusion.16
  525.1 0.3 multiply_reduce_fusion.2
  525.6 4.9 fusion.16
  530.5 0.3 multiply_reduce_fusion.2
  531.1 4.9 fusion.16
  536.0 0.3 multiply_reduce_fusion.2
  536.5 4.9 fusion.16
  541.4 0.3 multiply_reduce_fusion.2
  542.0 4.9 fusion.16
  546.9 0.3 multiply_reduce_fusion.2
  547.4 78.8 %pmax.7 = f32[2048]{0:T(1024)S(1)} all-reduce(f32[2048]{0:T(1024)S(1)} %bitcast.47), channel_id=1, replica_groups=mesh['req'=64,'tp'=4] {'req','tp'}, use_global_device_ids=true, to_apply=%region_8.9 | all-reduce | flops 2048 | bytes 16384 | tf_op jit(solution)/shard_map/pmax | solution.py:58
  626.3 73.9 %all-reduce.1 = (f32[2048]{0:T(1024)S(1)}, f32[2048]{0:T(1024)S(1)}, f32[2048]{0:T(1024)S(1)}) all-reduce(f32[2048]{0:T(1024)S(1)} %bitcast.49, f32[2048]{0:T(1024)S(1)} %get-tuple-element.85, f32[2048]{0:T(1024)S(1)} %get-tuple-element.84), channel_id=1, replica_groups=mesh['req'=64,'tp'=4] {'req','tp'}, use_global_device_ids=true, to_apply=%region_7.8 | all-reduce | flops 6144 | bytes 49152 | tf_op jit(solution)/shard_map/psum | solution.py:60
  700.2 0.1 reshape.43
  700.2 0.1 reshape.45
  700.3 0.5 compare_select_fusion
  (61 shorter events, 1.5 us)
Async XLA Ops:
  21.0 14.6 %copy-start = (s32[64]{0:T(128)S(1)}, s32[64]{0:T(128)}, u32[]{:S(2)}) copy-start(s32[64]{0:T(128)} %param.13) | copy-start | bytes 772
  21.0 16.6 %copy-start.2 = (u32[256]{0:T(256)S(1)}, u32[256]{0:T(256)}, u32[]{:S(2)}) copy-start(u32[256]{0:T(256)} %constant.54) | copy-start | bytes 3076
  21.0 17.8 %copy-start.1 = (s32[32]{0:T(128)S(1)}, s32[32]{0:T(128)}, u32[]{:S(2)}) copy-start(s32[32]{0:T(128)} %param.11) | copy-start | bytes 388
  21.0 482.8 %all-to-all-start = ((bf16[64,32,5120]{2,1,0:T(8,128)(2,1)}), bf16[64,32,5120]{2,1,0:T(8,128)(2,1)}, u32[]{:S(2)}, u32[]{:S(2)}) async-start(bf16[64,32,5120]{2,1,0:T(8,128)(2,1)} %stack.2), calls=%async_computation | async-start | bytes 41943040 | tf_op jit(solution)/shard_map/all_to_all | solution.py:11
